TPU v7x, 512 devices: a whole 4x8x8 slice. The times are simulated.
512 devices in a mesh: energy: 8 (over y_lo, core), atom: 64 (over y_hi, x, z).
Axes of the slice: x: 4, y: 8 (y_hi: 2, y_lo: 4; y = y_hi * 4 + y_lo), z: 8, core: 2. Of those that a mesh axis runs over, the one named last changes fastest.
Arguments:
- green: bfloat16 [8, 64, 2, 512, 512], P('energy', 'atom'), may hold values from -0.25 to 0.25
- t_ref: bfloat16 [8, 64, 2, 32, 32], P('energy'), may hold values from -0.24748737 to 0.24748737
- radial: bfloat16 [8, 32, 1024], P('energy'), may hold values from -1 to 1
- energy_weight: float32 [8], P('energy'), may hold values from 10 to 60
- potential: float32 [64, 25, 1024], P('atom'), may hold values from -6 to 6
- coupling: float32 [25, 32], replicated, may hold values from -1 to 1
- zone: int32 [64, 15], P('atom'), may hold values from 0 to 63, as said below
- order: int32 [64], replicated, may hold values from 0 to 63, as said below
Outputs:
- mixed: float32 [64, 25, 1024], P('atom')
- final_density: float32 [64, 25, 1024], P('atom')
Inputs may be any that keep to these rules, and one draw needn't show every extreme that they name: `zone`: each row lists 16 - 1 distinct atom ids, none of them the atom at that row's position. `order`: A permutation of the atom ids.
All inputs are finite; a program needn't handle non-finite values.
Results may differ from a plain program's by a relative error of at most 0.035.
Values may be sent and summed in bfloat16 or wider, within the bound.
A program may use at most 64 MiB of HBM per device.

v0:
```python
import jax
import jax.numpy as jnp
from jax import lax
from jax.sharding import PartitionSpec as P

NITER = 4
MIXING = 0.5
STEEPNESS = 0.8


def drive_scale(field, basis, coupling):
    squares = basis.astype(jnp.float32) ** 2
    intersection = jnp.einsum("acr,br->acb", field, squares, precision=lax.Precision.HIGHEST)
    drive = jnp.einsum("acb,cb->ab", intersection, coupling, precision=lax.Precision.HIGHEST)
    return 1.0 + STEEPNESS * jnp.tanh(drive)


def scatter(zone_t, greens, channels):
    count = zone_t.shape[0]
    zone_size = zone_t.shape[1]
    order_size = zone_size * channels
    seed_block = jnp.concatenate([zone_t[:, 0, 0], zone_t[:, 0, 1]], -1).astype(jnp.float32)
    start = (
        jnp.zeros((count, zone_size, channels, 2 * channels), jnp.float32).at[:, 0].set(seed_block)
    )
    stacked = greens.reshape(count, 2 * order_size, order_size)
    iterate = start
    for sweep in range(NITER):
        current = iterate.astype(jnp.bfloat16).reshape(count, order_size, 2 * channels)
        product = jnp.einsum("aij,ajk->aik", stacked, current, preferred_element_type=jnp.float32)
        product = product.reshape(count, 2, zone_size, channels, 2 * channels)
        real_part = product[:, 0, :, :, :channels] - product[:, 1, :, :, channels:]
        imag_part = product[:, 0, :, :, channels:] + product[:, 1, :, :, :channels]
        scattered = jnp.concatenate([real_part, imag_part], -1).astype(jnp.bfloat16)
        left = jnp.einsum(
            "azbc,azcd->azbd", zone_t[:, :, 0], scattered, preferred_element_type=jnp.float32
        )
        right = jnp.einsum(
            "azbc,azcd->azbd", zone_t[:, :, 1], scattered, preferred_element_type=jnp.float32
        )
        update = jnp.concatenate(
            [
                left[..., :channels] - right[..., channels:],
                left[..., channels:] + right[..., :channels],
            ],
            -1,
        )
        iterate = start + update
    return iterate[:, 0, :, channels:]


def density(imag_tau, basis, coupling, weight):
    radial_f = basis.astype(jnp.float32)
    mixed_rows = jnp.einsum("aij,jr->air", imag_tau, radial_f, precision=lax.Precision.HIGHEST)
    paired = radial_f[None] * mixed_rows
    return weight * jnp.einsum("ci,air->acr", coupling, paired, precision=lax.Precision.HIGHEST)


def summed(local_terms):
    return lax.psum(local_terms, "energy")


def body(green, t_ref, radial, energy_weight, potential, coupling, zone, order):
    count = potential.shape[0]
    total = order.shape[0]
    channels = coupling.shape[1]
    atom_rank = lax.axis_index("atom")
    index_list = jnp.arange(total, dtype=jnp.int32)
    position_of = jnp.zeros((total,), jnp.int32).at[order].set(index_list)
    own_positions = atom_rank * count + jnp.arange(count, dtype=jnp.int32)
    zone_pos = jnp.concatenate([own_positions[:, None], position_of[zone]], 1)
    base_all = t_ref[0]
    base_own = lax.dynamic_slice_in_dim(base_all, atom_rank * count, count, 0)
    basis = radial[0]
    weight = energy_weight[0]
    greens = green[0]

    def matrices(field):
        scale = drive_scale(field, basis, coupling)
        own_t = (scale[:, None, :, None] * base_own.astype(jnp.float32)).astype(jnp.bfloat16)
        every = lax.all_gather(own_t, "atom", axis=0, tiled=True)
        return every[zone_pos]

    def path_blocks(field):
        return scatter(matrices(field), greens, channels)

    def one_pass(field):
        return density(path_blocks(field), basis, coupling, weight)

    first = one_pass(potential)
    mixed = (1.0 - MIXING) * potential + MIXING * summed(first)
    final = summed(one_pass(mixed))
    return (mixed, final)


def solution(mesh):
    placed = (
        P("energy", "atom", None, None, None),
        P("energy", None, None, None, None),
        P("energy", None, None),
        P("energy"),
        P("atom", None, None),
        P(),
        P("atom", None),
        P(),
    )
    return jax.shard_map(
        body,
        mesh=mesh,
        in_specs=placed,
        out_specs=(P("atom", None, None), P("atom", None, None)),
        check_vma=False,
    )
```

profile of v0, /device:TPU:2, one launch (start us, length us, event | category | flops | bytes accessed | tf_op | source)
XLA Modules:
  0.0 634.7 jit_solution(14289547260079247878)
XLA Ops:
  7.2 0.8 fusion.69
  8.0 0.7 compare_select_fusion.2
  8.7 1.2 fusion.3
  9.9 0.8 scatter_custom_fusion
  10.6 0.7 gather_fusion
  11.6 0.5 copy.92
  12.2 203.8 %all_gather.6 = bf16[64,2,32,32]{3,2,1,0:T(8,128)(2,1)S(1)} all-gather(bf16[1,2,32,32]{3,2,1,0:T(8,128)(2,1)S(1)} %fusion.43), channel_id=1, replica_groups=mesh['energy'=8,'atom'=64] {'atom'}, dimensions={0}, use_global_device_ids=true | all-gather | bytes 266240 | tf_op jit(solution)/shard_map/all_gather | solution.py:81
  215.9 0.6 gather_fusion.1
  216.7 0.4 convolution_bitcast_fusion.23
  217.8 0.2 convolution_bitcast_fusion.22
  218.4 0.4 convolution_bitcast_fusion.20
  220.2 0.4 convolution_bitcast_fusion.17
  222.0 0.4 convolution_bitcast_fusion.14
  224.2 0.6 copy-done.1
  224.8 0.3 convolution_multiply_fusion.3
  225.1 0.5 copy-done.4
  225.5 0.9 fusion.1
  226.5 96.0 %all-reduce.5.cloned.1.call-done = f32[1,25,1024]{2,1,0:T(8,128)} async-done(((f32[1,25,1024]{2,1,0:T(8,128)}), f32[1,25,1024]{2,1,0:T(8,128)}) %all-reduce.5.cloned.1.call-update) | async-done | bytes 102416 | tf_op jit(solution)/shard_map/psum | solution.py:60
  322.5 0.9 fusion.21
  323.5 0.3 fusion.4
  323.8 195.4 %all_gather.7 = bf16[64,2,32,32]{3,2,1,0:T(8,128)(2,1)S(1)} all-gather(bf16[1,2,32,32]{3,2,1,0:T(8,128)(2,1)S(1)} %fusion.44), channel_id=1, replica_groups=mesh['energy'=8,'atom'=64] {'atom'}, dimensions={0}, use_global_device_ids=true | all-gather | bytes 266240 | tf_op jit(solution)/shard_map/all_gather | solution.py:81
  519.3 0.6 gather_fusion.2
  520.0 0.4 convolution_bitcast_fusion.11
  520.9 0.2 convolution_bitcast_fusion.9
  521.8 0.4 convolution_bitcast_fusion.8
  523.5 0.4 convolution_bitcast_fusion.5
  525.3 0.4 convolution_bitcast_fusion.2
  526.9 0.3 convolution_multiply_fusion.2
  527.1 0.9 fusion
  528.0 0.7 copy.77
  528.8 97.4 %all-reduce.7.cloned.1.call-done = f32[1,25,1024]{2,1,0:T(8,128)} async-done(((f32[1,25,1024]{2,1,0:T(8,128)}), f32[1,25,1024]{2,1,0:T(8,128)}) %all-reduce.7.cloned.1.call-update) | async-done | bytes 102416 | tf_op jit(solution)/shard_map/psum | solution.py:60
  626.2 1.7 copy.78
  (79 shorter events, 10.2 us)
Async XLA Ops:
  7.2 209.5 %copy-start = (bf16[1,1,2,512,512]{4,3,2,1,0:T(8,128)(2,1)S(1)}, bf16[1,1,2,512,512]{4,3,2,1,0:T(8,128)(2,1)}, u32[]{:S(2)}) copy-start(bf16[1,1,2,512,512]{4,3,2,1,0:T(8,128)(2,1)} %param.12) | copy-start | bytes 3145732
  7.2 4.2 copy-start.3
  7.2 315.3 %all-reduce.5.cloned.1.call-start = ((), (), s32[]{:S(2)}) async-start(), calls=%async_computation | async-start | bytes 262144 | tf_op jit(solution)/shard_map/psum | solution.py:60
  224.0 0.8 copy-start.1
  224.8 0.7 copy-start.4
  226.4 96.1 %copy-start.2 = (f32[1,25,1024]{2,0,1:T(1,128)S(1)}, f32[1,25,1024]{2,0,1:T(1,128)}, u32[]{:S(2)}) copy-start(f32[1,25,1024]{2,0,1:T(1,128)} %param.16) | copy-start | bytes 307204
  226.4 399.8 %all-reduce.7.cloned.1.call-start = ((), (), s32[]{:S(2)}) async-start(), calls=%async_computation.1 | async-start | bytes 262144 | tf_op jit(solution)/shard_map/psum | solution.py:60
Sparse Core Ops, SparseCore 0:
  226.6 95.9 all-reduce.4
  528.2 98.0 all-reduce.6
where the time goes:
time: 635 us
  blocking collectives  399 us (63%)
  waiting for transfers between devices  193 us (30%)
  between operations  15.2 us (2%)
  matrix products  11 us (2%)
  local copies, waits for them, and re-layouts  8.5 us (1%)
  other arithmetic  7.25 us (1%)
    all_gather x2, blocking collectives, matrices(): every = lax.all_gather(own_t, 'atom', axis=0, tiled=True)  399 us
    psum x2, waiting for transfers between devices, summed(): return lax.psum(local_terms, 'energy')  193 us
  transfers between devices with their start and end apart: 2, of which 2 were waited for; matrix products, arithmetic and copies ran while one was open for 0% of the time, Pallas kernels for 0%

commit v1 on v0

--- a/solution.py
+++ b/solution.py
@@ -6,6 +6,13 @@
 NITER = 4
 MIXING = 0.5
 STEEPNESS = 0.8
+
+
+def exchange_gather(x, mesh_axis, dim):
+    size = lax.axis_size(mesh_axis)
+    blocks = jnp.stack([x for _ in range(size)])
+    blocks = lax.all_to_all(blocks, mesh_axis, split_axis=0, concat_axis=0)
+    return jnp.concatenate(blocks, axis=dim)
 
 
 def drive_scale(field, basis, coupling):
@@ -78,7 +85,7 @@
     def matrices(field):
         scale = drive_scale(field, basis, coupling)
         own_t = (scale[:, None, :, None] * base_own.astype(jnp.float32)).astype(jnp.bfloat16)
-        every = lax.all_gather(own_t, "atom", axis=0, tiled=True)
+        every = exchange_gather(own_t, "atom", 0)
         return every[zone_pos]
 
     def path_blocks(field):

time: 635 us -> 243 us (0.38)
  blocking collectives: 399 us -> 27.3 us
  waiting for transfers between devices: 193 us -> 150 us
  starting transfers between devices: 0.08 us -> 19.2 us
    all_gather x2 -> x0, blocking collectives: 399 us -> none  [matrices(): every = lax.all_gather(own_t, 'atom', axis=0, tiled=True)]
    psum x2, waiting for transfers between devices: 193 us -> 138 us  [summed(): return lax.psum(local_terms, 'energy')]
    all_to_all x0 -> x1, blocking collectives: none -> 27.3 us  [exchange_gather(): blocks = lax.all_to_all(blocks, mesh_axis, split_axis=0, concat_axis=0)]
    all_to_all x0 -> x1, starting transfers between devices: none -> 19.1 us  [exchange_gather(): blocks = lax.all_to_all(blocks, mesh_axis, split_axis=0, concat_axis=0)]
    all_to_all x0 -> x1, waiting for transfers between devices: none -> 11.9 us  [exchange_gather(): blocks = lax.all_to_all(blocks, mesh_axis, split_axis=0, concat_axis=0)]
  transfers between devices with their start and end apart: 2 -> 3, of which waited for: 2 -> 3; matrix products, arithmetic and copies ran while one was open for 0% -> 1% of each run, Pallas kernels for 0% -> 0%
where the time goes in v1:
time: 243 us; the launch traced here: 242 us
  waiting for transfers between devices  150 us (62%)
  blocking collectives  27.3 us (11%)
  starting transfers between devices  19.2 us (8%)
  between operations  15.2 us (6%)
  local copies, waits for them, and re-layouts  13.8 us (6%)
  matrix products  11.2 us (5%)
  other arithmetic  5.82 us (2%)
    psum x2, waiting for transfers between devices, summed(): return lax.psum(local_terms, 'energy')  138 us
    all_to_all x1, blocking collectives, exchange_gather(): blocks = lax.all_to_all(blocks, mesh_axis, split_axis=0, concat_axis=0)  27.3 us
    all_to_all x1, starting transfers between devices, exchange_gather(): blocks = lax.all_to_all(blocks, mesh_axis, split_axis=0, concat_axis=0)  19.1 us
    all_to_all x1, waiting for transfers between devices, exchange_gather(): blocks = lax.all_to_all(blocks, mesh_axis, split_axis=0, concat_axis=0)  11.9 us
    unnamed x19, local copies, waits for them, and re-layouts  7.65 us
  transfers between devices with their start and end apart: 3, of which 3 were waited for; matrix products, arithmetic and copies ran while one was open for 1% of the time, Pallas kernels for 0%

profile of v1, /device:TPU:2, one launch (start us, length us, event | category | flops | bytes accessed | tf_op | source)
XLA Modules:
  0.0 242.3 jit_solution(16881262846047828272)
XLA Ops:
  7.2 1.2 fusion.3
  8.4 1.3 constant_dynamic-slice_fusion
  9.7 0.5 copy.92
  10.5 1.7 reshape.838
  12.2 19.1 %all-to-all-start = ((bf16[64,2,1024]{2,1,0:T(2,128)(2,1)}), bf16[64,2,1024]{2,1,0:T(2,128)(2,1)S(1)}, u32[]{:S(2)}, u32[]{:S(2)}) async-start(bf16[64,2,1024]{2,1,0:T(2,128)(2,1)} %reshape.838), calls=%async_computation | async-start | bytes 524288 | tf_op jit(solution)/shard_map/all_to_all | solution.py:14
  32.1 0.8 scatter_custom_fusion
  32.9 0.7 gather_fusion
  33.6 11.9 %all-to-all-done = bf16[64,2,1024]{2,1,0:T(2,128)(2,1)S(1)} async-done(((bf16[64,2,1024]{2,1,0:T(2,128)(2,1)}), bf16[64,2,1024]{2,1,0:T(2,128)(2,1)S(1)}, u32[]{:S(2)}, u32[]{:S(2)}) %all-to-all-start) | async-done | bytes 262176 | tf_op jit(solution)/shard_map/all_to_all | solution.py:14
  45.5 0.5 reshape.839
  46.0 0.6 gather_fusion.1
  46.8 0.4 convolution_bitcast_fusion.23
  48.5 0.4 convolution_bitcast_fusion.20
  50.3 0.4 convolution_bitcast_fusion.17
  52.1 0.4 convolution_bitcast_fusion.14
  53.7 0.6 copy-done.1
  54.5 0.4 copy-done.3
  55.0 0.9 fusion.1
  56.0 69.5 %all-reduce.5.cloned.1.call-done = f32[1,25,1024]{2,1,0:T(8,128)} async-done(((f32[1,25,1024]{2,1,0:T(8,128)}), f32[1,25,1024]{2,1,0:T(8,128)}) %all-reduce.5.cloned.1.call-update) | async-done | bytes 102416 | tf_op jit(solution)/shard_map/psum | solution.py:67
  125.5 0.9 fusion.21
  126.4 0.3 fusion.4
  127.1 1.0 reshape.840
  128.1 27.3 %all_to_all.10 = bf16[64,2,1024]{2,1,0:T(2,128)(2,1)S(1)} all-to-all(bf16[64,2,1024]{2,1,0:T(2,128)(2,1)S(1)} %reshape.840), channel_id=1, replica_groups=mesh['energy'=8,'atom'=64] {'atom'}, dimensions={0} | all-to-all | bytes 524288 | tf_op jit(solution)/shard_map/all_to_all | solution.py:14
  155.4 0.5 reshape.841
  155.9 0.6 gather_fusion.2
  156.6 0.4 convolution_bitcast_fusion.11
  158.4 0.4 convolution_bitcast_fusion.8
  160.2 0.4 convolution_bitcast_fusion.5
  161.9 0.4 convolution_bitcast_fusion.2
  163.8 0.9 fusion
  164.7 0.7 copy.77
  165.4 68.3 %all-reduce.7.cloned.1.call-done = f32[1,25,1024]{2,1,0:T(8,128)} async-done(((f32[1,25,1024]{2,1,0:T(8,128)}), f32[1,25,1024]{2,1,0:T(8,128)}) %all-reduce.7.cloned.1.call-update) | async-done | bytes 102416 | tf_op jit(solution)/shard_map/psum | solution.py:67
  233.8 1.7 copy.78
  (88 shorter events, 11.6 us)
Async XLA Ops:
  7.2 39.6 %copy-start = (bf16[1,1,2,512,512]{4,3,2,1,0:T(8,128)(2,1)S(1)}, bf16[1,1,2,512,512]{4,3,2,1,0:T(8,128)(2,1)}, u32[]{:S(2)}) copy-start(bf16[1,1,2,512,512]{4,3,2,1,0:T(8,128)(2,1)} %param.12) | copy-start | bytes 3145732
  12.2 33.3 %all-to-all-start = ((bf16[64,2,1024]{2,1,0:T(2,128)(2,1)}), bf16[64,2,1024]{2,1,0:T(2,128)(2,1)S(1)}, u32[]{:S(2)}, u32[]{:S(2)}) async-start(bf16[64,2,1024]{2,1,0:T(2,128)(2,1)} %reshape.838), calls=%async_computation | async-start | bytes 524288 | tf_op jit(solution)/shard_map/all_to_all | solution.py:14
  31.3 0.7 copy-start.4
  31.3 94.2 %all-reduce.5.cloned.1.call-start = ((), (), s32[]{:S(2)}) async-start(), calls=%async_computation.2 | async-start | bytes 262144 | tf_op jit(solution)/shard_map/psum | solution.py:67
  32.1 0.8 copy-start.5
  53.4 0.8 copy-start.1
  54.3 0.7 copy-start.3
  55.9 69.6 %copy-start.2 = (f32[1,25,1024]{2,0,1:T(1,128)S(1)}, f32[1,25,1024]{2,0,1:T(1,128)}, u32[]{:S(2)}) copy-start(f32[1,25,1024]{2,0,1:T(1,128)} %param.16) | copy-start | bytes 307204
  55.9 177.9 %all-reduce.7.cloned.1.call-start = ((), (), s32[]{:S(2)}) async-start(), calls=%async_computation.3 | async-start | bytes 262144 | tf_op jit(solution)/shard_map/psum | solution.py:67
Sparse Core Ops, SparseCore 0:
  56.1 69.3 all-reduce.4
  164.8 68.9 all-reduce.6

commit v2 on v0

--- a/solution.py
+++ b/solution.py
@@ -2,6 +2,7 @@
 import jax.numpy as jnp
 from jax import lax
 from jax.sharding import PartitionSpec as P
+from jax.lax import all_gather
 
 NITER = 4
 MIXING = 0.5
@@ -57,7 +58,7 @@
 
 
 def summed(local_terms):
-    return lax.psum(local_terms, "energy")
+    return jnp.sum(all_gather(local_terms, "energy"), axis=0)
 
 
 def body(green, t_ref, radial, energy_weight, potential, coupling, zone, order):

time: 635 us -> 514 us (0.81)
  the two profiles are of different devices: /device:TPU:2 before, /device:TPU:1 now
where the time goes in v2:
time: 514 us
  blocking collectives  488 us (95%)
  matrix products  9.79 us (2%)
  local copies, waits for them, and re-layouts  8 us (2%)
  other arithmetic  6.45 us (1%)
    all_gather x2, blocking collectives, matrices(): every = lax.all_gather(own_t, 'atom', axis=0, tiled=True)  399 us
    all_gather x2, blocking collectives, summed(): return jnp.sum(all_gather(local_terms, 'energy'), axis=0)  89.3 us

profile of v2, /device:TPU:1, one launch (start us, length us, event | category | flops | bytes accessed | tf_op | source)
XLA Modules:
  0.0 514.2 jit_solution(17348661613996198498)
XLA Ops:
  1.4 0.4 copy-done
  1.9 0.7 fusion.71
  2.5 0.7 compare_select_fusion.2
  3.2 1.2 fusion.3
  4.4 0.8 scatter_custom_fusion
  5.2 0.7 gather_fusion
  6.2 0.5 copy.84
  6.7 208.1 %all_gather.18 = bf16[64,2,32,32]{3,2,1,0:T(8,128)(2,1)S(1)} all-gather(bf16[1,2,32,32]{3,2,1,0:T(8,128)(2,1)S(1)} %fusion.45), channel_id=1, replica_groups=mesh['energy'=8,'atom'=64] {'atom'}, dimensions={0}, use_global_device_ids=true | all-gather | bytes 266240 | tf_op jit(solution)/shard_map/all_gather | solution.py:82
  214.9 0.6 gather_fusion.1
  215.6 0.4 convolution_bitcast_fusion.23
  216.5 0.2 convolution_bitcast_fusion.21
  216.7 0.2 convolution_bitcast_fusion.22
  217.4 0.4 convolution_bitcast_fusion.20
  219.1 0.4 convolution_bitcast_fusion.17
  220.9 0.4 convolution_bitcast_fusion.14
  222.5 0.6 copy-done.1
  223.1 0.3 convolution_multiply_fusion.3
  223.4 0.2 fusion.1
  223.6 44.9 %all-gather = f32[8,25,1024]{2,1,0:T(8,128)S(1)} all-gather(f32[1,25,1024]{2,1,0:T(8,128)S(1)} %fusion.1), channel_id=2, replica_groups=mesh['energy'=8,'atom'=64] {'energy'}, dimensions={0}, use_global_device_ids=true | all-gather | bytes 921600 | tf_op jit(solution)/shard_map/all_gather | solution.py:61
  268.6 0.8 copy-done.2
  269.5 0.3 fusion.4
  269.8 0.4 copy-done.3
  270.3 190.7 %all_gather.21 = bf16[64,2,32,32]{3,2,1,0:T(8,128)(2,1)S(1)} all-gather(bf16[1,2,32,32]{3,2,1,0:T(8,128)(2,1)S(1)} %fusion.46), channel_id=1, replica_groups=mesh['energy'=8,'atom'=64] {'atom'}, dimensions={0}, use_global_device_ids=true | all-gather | bytes 266240 | tf_op jit(solution)/shard_map/all_gather | solution.py:82
  460.9 0.6 gather_fusion.2
  461.7 0.4 convolution_bitcast_fusion.11
  463.4 0.4 convolution_bitcast_fusion.8
  465.2 0.4 convolution_bitcast_fusion.5
  467.0 0.4 convolution_bitcast_fusion.2
  468.5 0.3 convolution_multiply_fusion.2
  468.8 0.2 fusion
  469.0 44.4 %all-gather.1 = f32[8,25,1024]{2,1,0:T(8,128)S(1)} all-gather(f32[1,25,1024]{2,1,0:T(8,128)S(1)} %fusion), channel_id=3, replica_groups=mesh['energy'=8,'atom'=64] {'energy'}, dimensions={0}, use_global_device_ids=true | all-gather | bytes 921600 | tf_op jit(solution)/shard_map/all_gather | solution.py:61
  513.5 0.7 reduce_sum.25
  (78 shorter events, 10.4 us)
Async XLA Ops:
  0.6 1.2 copy-start
  0.6 2.5 copy-start.5
  0.7 5.3 %copy-start.4 = (bf16[1,64,2,32,32]{1,4,3,2,0:T(8,128)(2,1)S(1)}, bf16[1,64,2,32,32]{1,4,3,2,0:T(8,128)(2,1)}, u32[]{:S(2)}) copy-start(bf16[1,64,2,32,32]{1,4,3,2,0:T(8,128)(2,1)} %param.13) | copy-start | bytes 786436
  222.2 0.8 copy-start.1
  268.5 0.9 copy-start.2
  269.5 0.6 copy-start.3
